TPU v7x, 128 devices: a whole 4x4x4 slice. The times are simulated.
128 devices in a mesh: req: 32 (over x, z, core), ch: 4 (over y).
Axes of the slice: x: 4, y: 4, z: 4, core: 2. Of those that a mesh axis runs over, the one named last changes fastest.
Arguments:
- tokens: bfloat16 [49152, 2560], P('req'), may hold values from -6 to 6
- w_in: bfloat16 [2560, 2560], P(None, 'ch'), may hold values from -0.125 to 0.125
- w_gate: bfloat16 [2560, 2560], P(None, 'ch'), may hold values from -0.125 to 0.125
- gate_a: bfloat16 [20, 128, 128], P('ch'), may hold values from -0.5 to 0.5
- gate_i: bfloat16 [20, 128, 128], P('ch'), may hold values from -0.5 to 0.5
- conv_w: float32 [4, 2560], P(None, 'ch'), may hold values from -3 to 3
- decay_rate: float32 [2560], P('ch'), may hold values from 9.765625e-06 to 0.04
- w_out: bfloat16 [2560, 2560], P('ch'), may hold values from -0.15625 to 0.15625
- cached_state: float32 [2048, 2560], P('req', 'ch'), may hold values from -3 to 3
- cached_inputs: bfloat16 [2048, 3, 2560], P('req', None, 'ch'), may hold values from -6 to 6
- span_lengths: int32 [16], replicated, may hold values from 1 to 2048, 16384 in all
- accepted: int32 [2048], P('req'), may hold values from 1 to 16
- owner: int32 [2048, 1], P('req'), may hold values from 0 to 31; in each aligned block of 64 rows (0 to 63, 64 to 127, ...) at most 4 rows name the same one
Outputs:
- mixed: bfloat16 [49152, 2560], P('req', 'ch')
- owned_state: float32 [32, 128, 2560], P('req', None, 'ch')
- owned_inputs: bfloat16 [32, 128, 3, 2560], P('req', None, None, 'ch')
Inputs may be any that keep to these rules, and one draw needn't show every extreme that they name: Among the 64 requests of one block no owner is named more than 4 times, a bound that some block reaches. `span_lengths`: the lengths sum to 16384; the longest is exactly 2048.
All inputs are finite; a program needn't handle non-finite values.
Results may differ from a plain program's by a relative error of at most 0.0095.
Values may be sent and summed in bfloat16 or wider, within the bound.
A program may use at most 128 MiB of HBM per device.

v0:
```python
import functools

import jax
import jax.numpy as jnp
from jax import lax
from jax.experimental import pallas as pl
from jax.experimental.pallas import tpu as pltpu
from jax.sharding import PartitionSpec as P

CONV = 4
HIST = CONV - 1
DRAFT = 16
SPAN_ROWS = 512
BLOCK = 128
CHUNK = 128
HALF = CHUNK // 2
GROUP = CHUNK // DRAFT
HALO = 16
BACK = 4
MESH = pl.DeviceIdType.MESH
F32 = jnp.float32
BF16 = jnp.bfloat16
SERIES = (0.99999999, -0.49999941, 0.16665585, -0.04159356, 0.00810764, -0.00105947)


def lanes(b):
    return pl.ds(pl.multiple_of(b * BLOCK, BLOCK), BLOCK)


def rows_of(c, count):
    return pl.ds(pl.multiple_of(c * count, count), count)


def kernel(
    lag,
    n_req,
    n_ch,
    span_ref,
    accepted_ref,
    owner_ref,
    conv_ref,
    rate_ref,
    tokens_hbm,
    w_in_hbm,
    w_gate_hbm,
    gate_a_hbm,
    gate_i_hbm,
    w_out_hbm,
    state_hbm,
    cached_hbm,
    mixed_hbm,
    ostate_hbm,
    oin_hbm,
    w_cat,
    w_out,
    tok_d,
    tok_s,
    gw,
    state,
    cached,
    cached_f,
    proj,
    inner,
    branch,
    hidden,
    kept,
    acc_b,
    inner_s,
    branch_s,
    local,
    decays,
    ends_a,
    ends_h,
    sum_send,
    sum_recv,
    own,
    stash_r,
    stash_l,
    send_r,
    send_l,
    recv_l,
    recv_r,
    send2_r,
    send2_l,
    recv2_l,
    recv2_r,
    a2a_send,
    a2a_recv,
    mout,
    ost,
    oin,
    load_sem,
    tok_sem,
    halo_send_sem,
    halo_recv_sem,
    sum_send_sem,
    sum_recv_sem,
    one_send,
    one_recv,
    two_send,
    two_recv,
    a2a_send_sem,
    a2a_recv_sem,
    out_sem,
    end_sem,
):
    chans = w_in_hbm.shape[1]
    blocks = chans // BLOCK
    requests = accepted_ref.shape[1]
    slots = 2 * requests // n_req
    drafts = requests * DRAFT // CHUNK
    spans = SPAN_ROWS // CHUNK
    me = lax.axis_index("req")
    place = lax.axis_index("ch")
    right = lax.rem(place + 1, n_ch)
    left = lax.rem(place + n_ch - 1, n_ch)
    far = lax.rem(place + 2, n_ch)

    def peer(j):
        return lax.rem(me + j, n_req)

    loads = [
        pltpu.make_async_copy(w_in_hbm, w_cat.at[:, pl.ds(0, chans)], load_sem.at[0]),
        pltpu.make_async_copy(w_gate_hbm, w_cat.at[:, pl.ds(chans, chans)], load_sem.at[1]),
        pltpu.make_async_copy(gate_a_hbm, gw.at[:, :, pl.ds(0, BLOCK)], load_sem.at[2]),
        pltpu.make_async_copy(gate_i_hbm, gw.at[:, :, pl.ds(BLOCK, BLOCK)], load_sem.at[3]),
        pltpu.make_async_copy(state_hbm, state, load_sem.at[4]),
        pltpu.make_async_copy(cached_hbm, cached, load_sem.at[5]),
    ]
    for k, source in enumerate((place, right, far, left)):
        columns = pl.ds(pl.multiple_of(source * chans, BLOCK), chans)
        loads.append(
            pltpu.make_async_copy(
                w_out_hbm.at[:, columns], w_out.at[:, pl.ds(k * chans, chans)], load_sem.at[6 + k]
            )
        )

    def load_tokens(c):
        return pltpu.make_async_copy(
            tokens_hbm.at[pl.ds(pl.multiple_of(SPAN_ROWS + c * CHUNK, CHUNK), CHUNK)],
            tok_d.at[rows_of(c, CHUNK)],
            tok_sem.at[c],
        )

    load_span = pltpu.make_async_copy(
        tokens_hbm.at[pl.ds(0, SPAN_ROWS)], tok_s.at[pl.ds(HALO, SPAN_ROWS)], load_sem.at[10]
    )
    load_tokens(0).start()
    for copy in loads[:6]:
        copy.start()
    for copy in loads[6:]:
        copy.start()

    @pl.loop(1, drafts)
    def _(c):
        load_tokens(c).start()

    load_span.start()

    barrier = pltpu.get_barrier_semaphore()

    @pl.loop(1, n_req)
    def _(j):
        pl.semaphore_signal(barrier, inc=1, device_id={"req": peer(j)}, device_id_type=MESH)

    for side in (left, right):
        pl.semaphore_signal(barrier, inc=1, device_id={"ch": side}, device_id_type=MESH)

    def halo_copy():
        return pltpu.make_async_remote_copy(
            src_ref=tokens_hbm.at[pl.ds(SPAN_ROWS - HALO, HALO)],
            dst_ref=tok_s.at[pl.ds(0, HALO)],
            send_sem=halo_send_sem,
            recv_sem=halo_recv_sem,
            device_id={"req": peer(1)},
            device_id_type=MESH,
        )

    def first_copy(c, side):
        source, target, device = ((send_r, recv_l, right), (send_l, recv_r, left))[side]
        return pltpu.make_async_remote_copy(
            src_ref=source.at[c],
            dst_ref=target.at[c],
            send_sem=one_send.at[c, side],
            recv_sem=one_recv.at[c, side],
            device_id={"ch": device},
            device_id_type=MESH,
        )

    def second_copy(c, side):
        source, target, device = ((send2_r, recv2_l, right), (send2_l, recv2_r, left))[side]
        return pltpu.make_async_remote_copy(
            src_ref=source.at[c],
            dst_ref=target.at[c],
            send_sem=two_send.at[c, side],
            recv_sem=two_recv.at[c, side],
            device_id={"ch": device},
            device_id_type=MESH,
        )

    def a2a_copy(j):
        return pltpu.make_async_remote_copy(
            src_ref=a2a_send.at[peer(j)],
            dst_ref=a2a_recv.at[me],
            send_sem=a2a_send_sem.at[j],
            recv_sem=a2a_recv_sem.at[j],
            device_id={"req": peer(j)},
            device_id_type=MESH,
        )

    def sum_copy(j):
        return pltpu.make_async_remote_copy(
            src_ref=sum_send,
            dst_ref=sum_recv.at[j - 1],
            send_sem=sum_send_sem.at[j - 1],
            recv_sem=sum_recv_sem.at[j - 1],
            device_id={"req": peer(j)},
            device_id_type=MESH,
        )

    def spread_accepted():
        across = lax.broadcasted_iota(jnp.int32, (requests, requests), 1)
        down = lax.broadcasted_iota(jnp.int32, (requests, requests), 0)
        column = jnp.sum(
            jnp.where(across == down, accepted_ref[...], 0), axis=1, keepdims=True
        )
        acc_b[...] = jnp.broadcast_to(column, (requests, BLOCK))

    spread_accepted()

    firsts = [jnp.int32(0)]
    for i in range(span_ref.shape[0] - 1):
        firsts.append(firsts[-1] + span_ref[i])

    def project(tokens, count):
        for n in range(0, 2 * chans, 2 * BLOCK):
            proj[pl.ds(0, count), n : n + 2 * BLOCK] = jnp.dot(
                tokens, w_cat[:, n : n + 2 * BLOCK], preferred_element_type=F32
            )

    def gelu(u):
        return (0.5 * u) * (1.0 + jnp.tanh(u * (0.7978845608028654 + 0.035677408136300125 * (u * u))))

    def gates(conv, b):
        both = jnp.dot(conv.astype(BF16), gw[b], preferred_element_type=F32)
        rate_gate = 0.5 + 0.5 * jnp.tanh(0.5 * both[:, :BLOCK])
        input_gate = 0.5 + 0.5 * jnp.tanh(0.5 * both[:, BLOCK:])
        y = (16.0 * rate_ref[:, lanes(b)]) * rate_gate
        series = SERIES[-1]
        for term in SERIES[-2::-1]:
            series = series * y + term
        z = y * series
        drive = z * lax.rsqrt(jnp.maximum(z, 1e-37)) * input_gate * conv
        return jnp.exp(-0.5 * y), drive

    def spread():
        return jnp.concatenate([hidden[b] for b in range(blocks)], 1)

    def project_out(c, gated):
        def share(k):
            return jnp.dot(
                gated, w_out[:, k * chans : (k + 1) * chans], preferred_element_type=F32
            ).astype(BF16)

        part = share(2)
        send_r[c, pl.ds(0, HALF)] = part[:HALF]
        send_l[c, pl.ds(0, HALF)] = part[HALF:]
        part = share(1)
        stash_r[c] = part[:HALF]
        send_r[c, pl.ds(HALF, HALF)] = part[HALF:]
        first_copy(c, 0).start()
        part = share(3)
        send_l[c, pl.ds(HALF, HALF)] = part[:HALF]
        stash_l[c] = part[HALF:]
        first_copy(c, 1).start()
        own[c] = share(0)

    def pass_on(c):
        first_copy(c, 0).wait_recv()
        send2_r[c] = (recv_l[c, pl.ds(0, HALF)].astype(F32) + stash_r[c].astype(F32)).astype(BF16)
        second_copy(c, 0).start()
        first_copy(c, 1).wait_recv()
        send2_l[c] = (recv_r[c, pl.ds(0, HALF)].astype(F32) + stash_l[c].astype(F32)).astype(BF16)
        second_copy(c, 1).start()

    def out_copy(c):
        shift = jnp.where(c < drafts, SPAN_ROWS + c * CHUNK, (c - drafts) * CHUNK)
        return pltpu.make_async_copy(
            mout.at[rows_of(c, CHUNK)],
            mixed_hbm.at[pl.ds(pl.multiple_of(shift, CHUNK), CHUNK)],
            out_sem.at[c],
        )

    def finish(c):
        second_copy(c, 0).wait_recv()
        second_copy(c, 1).wait_recv()
        upper = own[c, pl.ds(0, HALF)].astype(F32) + recv2_l[c].astype(F32)
        lower = own[c, pl.ds(HALF, HALF)].astype(F32) + recv2_r[c].astype(F32)
        upper = upper + recv_r[c, pl.ds(HALF, HALF)].astype(F32)
        lower = lower + recv_l[c, pl.ds(HALF, HALF)].astype(F32)
        mout[rows_of(2 * c, HALF), :] = upper.astype(BF16)
        mout[rows_of(2 * c + 1, HALF), :] = lower.astype(BF16)
        out_copy(c).start()

    load_tokens(0).wait()
    for copy in loads[:6]:
        copy.wait()
    cached_f[...] = cached[...].astype(F32)

    @pl.loop(0, drafts)
    def _(c):
        @pl.when(c > 0)
        def _():
            load_tokens(c).wait()

        project(tok_d[rows_of(c, CHUNK), :], CHUNK)
        for b in range(blocks):
            inner[b] = proj[pl.ds(0, CHUNK), b * BLOCK : (b + 1) * BLOCK].astype(BF16).astype(F32)
        branch[...] = gelu(proj[pl.ds(0, CHUNK), chans:])
        members = rows_of(c, GROUP)
        accepted = acc_b[members, :]

        @pl.loop(0, blocks)
        def _(b):
            rows = [cached_f[j, members, lanes(b)] for j in range(HIST)]
            rows += [inner[b, pl.ds(t, GROUP, stride=DRAFT), :] for t in range(DRAFT)]
            x = jnp.concatenate(rows, 0)
            conv = 0.0
            for k in range(CONV):
                at = (HIST - k) * GROUP
                conv = conv + conv_ref[k : k + 1, lanes(b)] * x[at : at + CHUNK]
            decay, drive = gates(conv, b)
            h = state[members, lanes(b)]
            picked = [jnp.zeros((GROUP, BLOCK), F32) for _ in range(1 + HIST)]
            for t in range(DRAFT):
                part = slice(t * GROUP, (t + 1) * GROUP)
                h = decay[part] * h + drive[part]
                hidden[b, pl.ds(t, GROUP, stride=DRAFT), :] = h
                chosen = accepted == t + 1
                picked[0] = jnp.where(chosen, h, picked[0])
                for j in range(HIST):
                    picked[1 + j] = jnp.where(chosen, rows[t + 1 + j], picked[1 + j])
            for j in range(1 + HIST):
                kept[pl.ds(pl.multiple_of(j * requests + c * GROUP, GROUP), GROUP), lanes(b)] = picked[j]

        gated = (branch[...] * spread()).astype(BF16)

        @pl.when(c == 0)
        def _():
            for copy in loads[6:]:
                copy.wait()
            pl.semaphore_wait(barrier, n_req - 1 + 2)
            halo_copy().start()

        project_out(c, gated)

        @pl.when(c >= lag)
        def _():
            pass_on(c - lag)

    owner_row = owner_ref[...]
    across = lax.broadcasted_iota(jnp.int32, (requests, requests), 1)
    down = lax.broadcasted_iota(jnp.int32, (requests, requests), 0)
    owner_column = jnp.sum(jnp.where(across == down, owner_row, 0), axis=1, keepdims=True)
    same = jnp.where(owner_column == owner_row, 1, 0)
    rank_row = jnp.sum(jnp.where(down < across, same, 0), axis=0, keepdims=True)
    slot_row = owner_row * slots + rank_row
    kinds = 1 + HIST
    tall = n_req * kinds * slots
    item = lax.broadcasted_iota(jnp.int32, (tall, requests), 0)
    slot_of = (item // (kinds * slots)) * slots + item % slots
    kind_of = (item // slots) % kinds
    hit = jnp.where(slot_of == slot_row, 1.0, 0.0)
    total = jnp.zeros((tall, chans), F32)
    for j in range(kinds):
        pick = jnp.where(kind_of == j, hit, 0.0).astype(BF16)
        total = total + jnp.dot(
            pick,
            kept[pl.ds(j * requests, requests), :].astype(BF16),
            preferred_element_type=F32,
        )
    a2a_send[...] = total.astype(BF16).reshape(n_req, kinds * slots, chans)

    @pl.loop(1, n_req)
    def _(j):
        a2a_copy(j).start()

    local_copy = pltpu.make_async_copy(a2a_send.at[me], a2a_recv.at[me], a2a_send_sem.at[0])
    local_copy.start()

    load_span.wait()
    halo_copy().wait_recv()

    @pl.loop(0, 2 * chans // (2 * BLOCK))
    def _(n):
        at = pl.ds(pl.multiple_of(n * 2 * BLOCK, 2 * BLOCK), 2 * BLOCK)
        proj[:, at] = jnp.dot(tok_s[...], w_cat[:, at], preferred_element_type=F32)

    for b in range(blocks):
        inner_s[b] = proj[:, b * BLOCK : (b + 1) * BLOCK].astype(BF16).astype(F32)
    branch_s[...] = gelu(proj[pl.ds(HALO, SPAN_ROWS), chans:])

    @pl.loop(drafts - lag, drafts)
    def _(c):
        pass_on(c)

    step = lax.broadcasted_iota(jnp.int32, (CHUNK, BLOCK), 0)
    offset = (step % GROUP) * DRAFT + step // GROUP

    @pl.loop(0, spans)
    def _(q):
        position = me * SPAN_ROWS + q * CHUNK + offset
        begin = jnp.zeros((CHUNK, BLOCK), jnp.int32)
        for first in firsts:
            begin = jnp.where(first <= position, first, begin)
        age = position - begin

        @pl.loop(0, blocks)
        def _(b):
            base = HALO - HIST + q * CHUNK
            rows = [
                inner_s[b, pl.ds(base + i, GROUP, stride=DRAFT), :] for i in range(DRAFT + HIST)
            ]
            x = jnp.concatenate(rows, 0)
            conv = conv_ref[0:1, lanes(b)] * x[HIST * GROUP : HIST * GROUP + CHUNK]
            for k in range(1, CONV):
                at = (HIST - k) * GROUP
                conv = conv + jnp.where(age >= k, conv_ref[k : k + 1, lanes(b)] * x[at : at + CHUNK], 0.0)
            decay, drive = gates(conv, b)
            decay = jnp.where(age > 0, decay, 0.0)
            h = jnp.zeros((GROUP, BLOCK), F32)
            a = jnp.ones((GROUP, BLOCK), F32)
            for t in range(DRAFT):
                part = slice(t * GROUP, (t + 1) * GROUP)
                h = decay[part] * h + drive[part]
                a = decay[part] * a
                at = pl.ds(pl.multiple_of(q * CHUNK + t * GROUP, GROUP), GROUP)
                local[at, lanes(b)] = h
                decays[at, lanes(b)] = a
            ends_a[rows_of(q, GROUP), lanes(b)] = a
            ends_h[rows_of(q, GROUP), lanes(b)] = h

    def link(s, carry):
        product, value = carry
        at = pl.ds(s, 1)
        a = ends_a[at, :]
        h = ends_h[at, :]
        ends_a[at, :] = product
        ends_h[at, :] = value
        return (a * product, a * value + h)

    product, value = lax.fori_loop(
        0, spans * GROUP, link, (jnp.ones((1, chans), F32), jnp.zeros((1, chans), F32))
    )
    sum_send[...] = jnp.zeros_like(sum_send)
    sum_send[0:1, :] = product
    sum_send[1:2, :] = value
    for j in range(1, BACK + 1):
        sum_copy(j).start()
    for j in range(1, BACK + 1):
        sum_copy(j).wait_recv()
    entering = sum_recv[BACK - 1, 1:2, :]
    for j in range(BACK - 2, -1, -1):
        entering = sum_recv[j, 0:1, :] * entering + sum_recv[j, 1:2, :]

    @pl.loop(0, spans)
    def _(q):
        carry = ends_h[rows_of(q, GROUP), :] + ends_a[rows_of(q, GROUP), :] * entering
        for t in range(DRAFT):
            at = pl.ds(pl.multiple_of(q * CHUNK + t * GROUP, GROUP), GROUP)
            h = local[at, :] + decays[at, :] * carry
            for b in range(blocks):
                hidden[b, pl.ds(t, GROUP, stride=DRAFT), :] = h[:, b * BLOCK : (b + 1) * BLOCK]
        project_out(drafts + q, (branch_s[rows_of(q, CHUNK), :] * spread()).astype(BF16))

        @pl.when(q >= lag)
        def _():
            pass_on(drafts + q - lag)

    local_copy.wait()

    @pl.loop(1, n_req)
    def _(j):
        a2a_copy(j).wait_recv()

    got = a2a_recv[...]
    ost[...] = got[:, :slots].astype(F32).reshape(n_req * slots, chans)
    for j in range(HIST):
        oin[j] = (
            got[:, (1 + j) * slots : (2 + j) * slots].astype(F32).reshape(n_req * slots, chans).astype(BF16)
        )
    ends = [
        pltpu.make_async_copy(ost, ostate_hbm, end_sem.at[0]),
        pltpu.make_async_copy(oin, oin_hbm, end_sem.at[1]),
    ]
    for copy in ends:
        copy.start()

    @pl.loop(drafts + max(spans - lag, 0), drafts + spans)
    def _(c):
        pass_on(c)

    @pl.loop(0, drafts + spans)
    def _(c):
        finish(c)

    halo_copy().wait_send()
    for j in range(1, BACK + 1):
        sum_copy(j).wait_send()

    @pl.loop(1, n_req)
    def _(j):
        a2a_copy(j).wait_send()

    @pl.loop(0, drafts + spans)
    def _(c):
        for side in range(2):
            first_copy(c, side).wait_send()
            second_copy(c, side).wait_send()
        out_copy(c).wait()

    for copy in ends:
        copy.wait()


def per_device(
    n_req,
    n_ch,
    tokens,
    w_in,
    w_gate,
    gate_a,
    gate_i,
    conv_w,
    decay_rate,
    w_out,
    cached_state,
    cached_inputs,
    span_lengths,
    accepted,
    owner,
):
    rows, width = tokens.shape
    chans = w_in.shape[1]
    blocks = chans // BLOCK
    requests = accepted.shape[0]
    slots = 2 * requests // n_req
    kinds = 1 + HIST
    drafts = requests * DRAFT // CHUNK
    spans = SPAN_ROWS // CHUNK
    chunks = drafts + spans
    lag = min(3, spans)
    vmem, anywhere, smem = (
        pl.BlockSpec(memory_space=pltpu.VMEM),
        pl.BlockSpec(memory_space=pl.ANY),
        pl.BlockSpec(memory_space=pltpu.SMEM),
    )
    dma = pltpu.SemaphoreType.DMA
    mixed, ostate, oin = pl.pallas_call(
        functools.partial(kernel, lag, n_req, n_ch),
        out_shape=(
            jax.ShapeDtypeStruct((rows, chans), BF16),
            jax.ShapeDtypeStruct((n_req * slots, chans), F32),
            jax.ShapeDtypeStruct((HIST, n_req * slots, chans), BF16),
        ),
        in_specs=[smem, vmem, vmem, vmem, vmem] + [anywhere] * 8,
        out_specs=(anywhere, anywhere, anywhere),
        scratch_shapes=[
            pltpu.VMEM((width, 2 * chans), BF16),
            pltpu.VMEM((chans, n_ch * chans), BF16),
            pltpu.VMEM((drafts * CHUNK, width), BF16),
            pltpu.VMEM((HALO + SPAN_ROWS, width), BF16),
            pltpu.VMEM((blocks, BLOCK, 2 * BLOCK), BF16),
            pltpu.VMEM((requests, chans), F32),
            pltpu.VMEM((HIST, requests, chans), BF16),
            pltpu.VMEM((HIST, requests, chans), F32),
            pltpu.VMEM((HALO + SPAN_ROWS, 2 * chans), F32),
            pltpu.VMEM((blocks, CHUNK, BLOCK), F32),
            pltpu.VMEM((CHUNK, chans), F32),
            pltpu.VMEM((blocks, CHUNK, BLOCK), F32),
            pltpu.VMEM((kinds * requests, chans), F32),
            pltpu.VMEM((requests, BLOCK), jnp.int32),
            pltpu.VMEM((blocks, HALO + SPAN_ROWS, BLOCK), F32),
            pltpu.VMEM((SPAN_ROWS, chans), F32),
            pltpu.VMEM((SPAN_ROWS, chans), F32),
            pltpu.VMEM((SPAN_ROWS, chans), F32),
            pltpu.VMEM((spans * GROUP, chans), F32),
            pltpu.VMEM((spans * GROUP, chans), F32),
            pltpu.VMEM((8, chans), F32),
            pltpu.VMEM((BACK, 8, chans), F32),
            pltpu.VMEM((chunks, CHUNK, chans), BF16),
            pltpu.VMEM((chunks, HALF, chans), BF16),
            pltpu.VMEM((chunks, HALF, chans), BF16),
            pltpu.VMEM((chunks, CHUNK, chans), BF16),
            pltpu.VMEM((chunks, CHUNK, chans), BF16),
            pltpu.VMEM((chunks, CHUNK, chans), BF16),
            pltpu.VMEM((chunks, CHUNK, chans), BF16),
            pltpu.VMEM((chunks, HALF, chans), BF16),
            pltpu.VMEM((chunks, HALF, chans), BF16),
            pltpu.VMEM((chunks, HALF, chans), BF16),
            pltpu.VMEM((chunks, HALF, chans), BF16),
            pltpu.VMEM((n_req, kinds * slots, chans), BF16),
            pltpu.VMEM((n_req, kinds * slots, chans), BF16),
            pltpu.VMEM((rows, chans), BF16),
            pltpu.VMEM((n_req * slots, chans), F32),
            pltpu.VMEM((HIST, n_req * slots, chans), BF16),
            dma((11,)),
            dma((drafts,)),
            dma,
            dma,
            dma((BACK,)),
            dma((BACK,)),
            dma((chunks, 2)),
            dma((chunks, 2)),
            dma((chunks, 2)),
            dma((chunks, 2)),
            dma((n_req,)),
            dma((n_req,)),
            dma((chunks,)),
            dma((2,)),
        ],
        compiler_params=pltpu.CompilerParams(
            collective_id=0, has_side_effects=True, vmem_limit_bytes=60 * 1024 * 1024
        ),
        name="griffin",
    )(
        span_lengths,
        accepted.reshape(1, requests),
        owner.reshape(1, requests),
        conv_w,
        decay_rate.reshape(1, chans),
        tokens,
        w_in,
        w_gate,
        gate_a,
        gate_i,
        w_out,
        cached_state,
        jnp.transpose(cached_inputs, (1, 0, 2)),
    )
    return (
        mixed,
        ostate.reshape(1, n_req * slots, chans),
        jnp.transpose(oin, (1, 0, 2)).reshape(1, n_req * slots, HIST, chans),
    )


def solution(mesh):
    return jax.shard_map(
        functools.partial(per_device, mesh.shape["req"], mesh.shape["ch"]),
        mesh=mesh,
        in_specs=(
            P("req", None),
            P(None, "ch"),
            P(None, "ch"),
            P("ch", None, None),
            P("ch", None, None),
            P(None, "ch"),
            P("ch"),
            P("ch", None),
            P("req", "ch"),
            P("req", None, "ch"),
            P(),
            P("req"),
            P("req", None),
        ),
        out_specs=(P("req", "ch"), P("req", None, "ch"), P("req", None, None, "ch")),
        check_vma=False,
    )
```

profile of v0, /device:TPU:1, one launch (start us, length us, event | category | flops | bytes accessed | tf_op | source)
XLA Modules:
  0.0 93.3 jit_solution(14676159093674048161)
XLA Ops:
  0.6 1.3 %reshape.23.rate_ref = f32[1,640]{1,0:T(1,128)} reshape(f32[640]{0:T(1024)} %param.19) | data formatting | bytes 5120 | tf_op jit(solution)/shard_map/reshape | solution.py:631
  1.9 86.8 %griffin.1 = (bf16[1536,640]{1,0:T(8,128)(2,1)}, f32[128,640]{1,0:T(8,128)}, bf16[3,128,640]{2,1,0:T(8,128)(2,1)}) custom-call(s32[16]{0:T(128)} %span_ref.1, s32[1,64]{1,0:T(1,128)} %bitcast.10, s32[1,64]{1,0:T(1,128)} %bitcast.11, f32[4,640]{1,0:T(4,128)} %conv_ref.1, f32[1,640]{1,0:T(1,128)} %reshape.23.rate_ref, bf16[1536,2560]{1,0:T(8,128)(2,1)} %tokens_hbm.1, ...), custom_call_target="tpu_custom_call" | custom-call | tf_op jit(solution)/shard_map/griffin/pallas_call | solution.py:559
  88.7 0.0 copy-start.1
  88.7 0.0 copy-start
  88.7 3.1 %copy.19 = bf16[1536,640]{1,0:T(8,128)(2,1)} copy(bf16[1536,640]{1,0:T(8,128)(2,1)} %get-tuple-element.12) | data formatting | bytes 3932160
  91.7 0.0 copy-done.1
  91.7 0.7 copy.20
  92.5 0.0 copy-done
  92.5 0.8 copy.21
Async XLA Ops:
  88.7 3.1 %copy-start.1 = (f32[128,640]{1,0:T(8,128)S(1)}, f32[128,640]{1,0:T(8,128)}, u32[]{:S(2)}) copy-start(f32[128,640]{1,0:T(8,128)} %get-tuple-element.7) | copy-start | bytes 983044
  88.7 3.8 %copy-start = (bf16[3,128,640]{2,1,0:T(8,128)(2,1)S(1)}, bf16[3,128,640]{2,1,0:T(8,128)(2,1)}, u32[]{:S(2)}) copy-start(bf16[3,128,640]{2,1,0:T(8,128)(2,1)} %get-tuple-element.8) | copy-start | bytes 1474564
where the time goes:
time: 93.5 us; the launch traced here: 93.3 us
  Pallas kernels  86.8 us (93%)
  local copies, waits for them, and re-layouts  5.84 us (6%)
    pallas_call x1, Pallas kernels, per_device(): pl.pallas_call(functools.partial(kernel, lag, n_req, n_ch), out_shape=(ja...  86.8 us
    unnamed x7, local copies, waits for them, and re-layouts  4.57 us

commit v1 on v0

--- a/solution.py
+++ b/solution.py
@@ -12,6 +12,7 @@
 DRAFT = 16
 SPAN_ROWS = 512
 BLOCK = 128
+WIDE = 256
 CHUNK = 128
 HALF = CHUNK // 2
 GROUP = CHUNK // DRAFT
@@ -48,13 +49,12 @@
     w_out_hbm,
     state_hbm,
     cached_hbm,
-    mixed_hbm,
-    ostate_hbm,
-    oin_hbm,
+    mout,
+    ost,
+    oin,
     w_cat,
     w_out,
-    tok_d,
-    tok_s,
+    tok,
     gw,
     state,
     cached,
@@ -86,10 +86,9 @@
     recv2_r,
     a2a_send,
     a2a_recv,
-    mout,
-    ost,
-    oin,
+    rates,
     load_sem,
+    w_sem,
     tok_sem,
     halo_send_sem,
     halo_recv_sem,
@@ -101,8 +100,6 @@
     two_recv,
     a2a_send_sem,
     a2a_recv_sem,
-    out_sem,
-    end_sem,
 ):
     chans = w_in_hbm.shape[1]
     blocks = chans // BLOCK
@@ -110,6 +107,7 @@
     slots = 2 * requests // n_req
     drafts = requests * DRAFT // CHUNK
     spans = SPAN_ROWS // CHUNK
+    wides = 2 * chans // WIDE
     me = lax.axis_index("req")
     place = lax.axis_index("ch")
     right = lax.rem(place + 1, n_ch)
@@ -119,43 +117,51 @@
     def peer(j):
         return lax.rem(me + j, n_req)
 
-    loads = [
-        pltpu.make_async_copy(w_in_hbm, w_cat.at[:, pl.ds(0, chans)], load_sem.at[0]),
-        pltpu.make_async_copy(w_gate_hbm, w_cat.at[:, pl.ds(chans, chans)], load_sem.at[1]),
-        pltpu.make_async_copy(gate_a_hbm, gw.at[:, :, pl.ds(0, BLOCK)], load_sem.at[2]),
-        pltpu.make_async_copy(gate_i_hbm, gw.at[:, :, pl.ds(BLOCK, BLOCK)], load_sem.at[3]),
-        pltpu.make_async_copy(state_hbm, state, load_sem.at[4]),
-        pltpu.make_async_copy(cached_hbm, cached, load_sem.at[5]),
+    def load_weights(n):
+        pieces = []
+        for k, source in enumerate((w_in_hbm, w_gate_hbm)):
+            low, high = max(n * WIDE, k * chans), min((n + 1) * WIDE, (k + 1) * chans)
+            if low < high:
+                pieces.append(
+                    pltpu.make_async_copy(
+                        source.at[:, pl.ds(low - k * chans, high - low)],
+                        w_cat.at[:, pl.ds(low, high - low)],
+                        w_sem.at[n, k],
+                    )
+                )
+        return pieces
+
+    small = [
+        pltpu.make_async_copy(gate_a_hbm, gw.at[:, :, pl.ds(0, BLOCK)], load_sem.at[0]),
+        pltpu.make_async_copy(gate_i_hbm, gw.at[:, :, pl.ds(BLOCK, BLOCK)], load_sem.at[1]),
+        pltpu.make_async_copy(state_hbm, state, load_sem.at[2]),
+        pltpu.make_async_copy(cached_hbm, cached, load_sem.at[3]),
     ]
-    for k, source in enumerate((place, right, far, left)):
+    load_out = []
+    for k, source in enumerate((far, right, left, place)):
         columns = pl.ds(pl.multiple_of(source * chans, BLOCK), chans)
-        loads.append(
+        load_out.append(
             pltpu.make_async_copy(
-                w_out_hbm.at[:, columns], w_out.at[:, pl.ds(k * chans, chans)], load_sem.at[6 + k]
+                w_out_hbm.at[:, columns], w_out.at[:, pl.ds(k * chans, chans)], load_sem.at[4 + k]
             )
         )
 
-    def load_tokens(c):
+    def load_tokens(i):
         return pltpu.make_async_copy(
-            tokens_hbm.at[pl.ds(pl.multiple_of(SPAN_ROWS + c * CHUNK, CHUNK), CHUNK)],
-            tok_d.at[rows_of(c, CHUNK)],
-            tok_sem.at[c],
-        )
-
-    load_span = pltpu.make_async_copy(
-        tokens_hbm.at[pl.ds(0, SPAN_ROWS)], tok_s.at[pl.ds(HALO, SPAN_ROWS)], load_sem.at[10]
-    )
-    load_tokens(0).start()
-    for copy in loads[:6]:
+            tokens_hbm.at[rows_of(i, CHUNK)],
+            tok.at[pl.ds(pl.multiple_of(HALO + i * CHUNK, HALO), CHUNK)],
+            tok_sem.at[i],
+        )
+
+    def token_rows(i):
+        return tok[pl.ds(pl.multiple_of(HALO + i * CHUNK, HALO), CHUNK), :]
+
+    load_tokens(spans).start()
+    for n in range(wides):
+        for copy in load_weights(n):
+            copy.start()
+    for copy in small:
         copy.start()
-    for copy in loads[6:]:
-        copy.start()
-
-    @pl.loop(1, drafts)
-    def _(c):
-        load_tokens(c).start()
-
-    load_span.start()
 
     barrier = pltpu.get_barrier_semaphore()
 
@@ -169,7 +175,7 @@
     def halo_copy():
         return pltpu.make_async_remote_copy(
             src_ref=tokens_hbm.at[pl.ds(SPAN_ROWS - HALO, HALO)],
-            dst_ref=tok_s.at[pl.ds(0, HALO)],
+            dst_ref=tok.at[pl.ds(0, HALO)],
             send_sem=halo_send_sem,
             recv_sem=halo_recv_sem,
             device_id={"req": peer(1)},
@@ -232,11 +238,9 @@
     for i in range(span_ref.shape[0] - 1):
         firsts.append(firsts[-1] + span_ref[i])
 
-    def project(tokens, count):
-        for n in range(0, 2 * chans, 2 * BLOCK):
-            proj[pl.ds(0, count), n : n + 2 * BLOCK] = jnp.dot(
-                tokens, w_cat[:, n : n + 2 * BLOCK], preferred_element_type=F32
-            )
+    def project(tokens, n):
+        at = slice(n * WIDE, (n + 1) * WIDE)
+        proj[:, at] = jnp.dot(tokens, w_cat[:, at], preferred_element_type=F32)
 
     def gelu(u):
         return (0.5 * u) * (1.0 + jnp.tanh(u * (0.7978845608028654 + 0.035677408136300125 * (u * u))))
@@ -245,7 +249,7 @@
         both = jnp.dot(conv.astype(BF16), gw[b], preferred_element_type=F32)
         rate_gate = 0.5 + 0.5 * jnp.tanh(0.5 * both[:, :BLOCK])
         input_gate = 0.5 + 0.5 * jnp.tanh(0.5 * both[:, BLOCK:])
-        y = (16.0 * rate_ref[:, lanes(b)]) * rate_gate
+        y = rates[0:1, lanes(b)] * rate_gate
         series = SERIES[-1]
         for term in SERIES[-2::-1]:
             series = series * y + term
@@ -257,23 +261,22 @@
         return jnp.concatenate([hidden[b] for b in range(blocks)], 1)
 
     def project_out(c, gated):
-        def share(k):
-            return jnp.dot(
-                gated, w_out[:, k * chans : (k + 1) * chans], preferred_element_type=F32
-            ).astype(BF16)
-
-        part = share(2)
-        send_r[c, pl.ds(0, HALF)] = part[:HALF]
-        send_l[c, pl.ds(0, HALF)] = part[HALF:]
-        part = share(1)
-        stash_r[c] = part[:HALF]
-        send_r[c, pl.ds(HALF, HALF)] = part[HALF:]
+        def shares(k):
+            at = slice(k * chans, (k + 2) * chans)
+            both = jnp.dot(gated, w_out[:, at], preferred_element_type=F32)
+            return both[:, :chans].astype(BF16), both[:, chans:].astype(BF16)
+
+        to_far, to_right = shares(0)
+        send_r[c, pl.ds(0, HALF)] = to_far[:HALF]
+        send_l[c, pl.ds(0, HALF)] = to_far[HALF:]
+        stash_r[c] = to_right[:HALF]
+        send_r[c, pl.ds(HALF, HALF)] = to_right[HALF:]
         first_copy(c, 0).start()
-        part = share(3)
-        send_l[c, pl.ds(HALF, HALF)] = part[:HALF]
-        stash_l[c] = part[HALF:]
+        to_left, to_own = shares(2)
+        send_l[c, pl.ds(HALF, HALF)] = to_left[:HALF]
+        stash_l[c] = to_left[HALF:]
         first_copy(c, 1).start()
-        own[c] = share(0)
+        own[c] = to_own
 
     def pass_on(c):
         first_copy(c, 0).wait_recv()
@@ -283,14 +286,6 @@
         send2_l[c] = (recv_r[c, pl.ds(0, HALF)].astype(F32) + stash_l[c].astype(F32)).astype(BF16)
         second_copy(c, 1).start()
 
-    def out_copy(c):
-        shift = jnp.where(c < drafts, SPAN_ROWS + c * CHUNK, (c - drafts) * CHUNK)
-        return pltpu.make_async_copy(
-            mout.at[rows_of(c, CHUNK)],
-            mixed_hbm.at[pl.ds(pl.multiple_of(shift, CHUNK), CHUNK)],
-            out_sem.at[c],
-        )
-
     def finish(c):
         second_copy(c, 0).wait_recv()
         second_copy(c, 1).wait_recv()
@@ -298,30 +293,89 @@
         lower = own[c, pl.ds(HALF, HALF)].astype(F32) + recv2_r[c].astype(F32)
         upper = upper + recv_r[c, pl.ds(HALF, HALF)].astype(F32)
         lower = lower + recv_l[c, pl.ds(HALF, HALF)].astype(F32)
-        mout[rows_of(2 * c, HALF), :] = upper.astype(BF16)
-        mout[rows_of(2 * c + 1, HALF), :] = lower.astype(BF16)
-        out_copy(c).start()
-
-    load_tokens(0).wait()
-    for copy in loads[:6]:
-        copy.wait()
-    cached_f[...] = cached[...].astype(F32)
-
-    @pl.loop(0, drafts)
-    def _(c):
-        @pl.when(c > 0)
-        def _():
-            load_tokens(c).wait()
-
-        project(tok_d[rows_of(c, CHUNK), :], CHUNK)
+        base = jnp.where(c < drafts, SPAN_ROWS + c * CHUNK, (c - drafts) * CHUNK)
+        mout[pl.ds(pl.multiple_of(base, HALF), HALF), :] = upper.astype(BF16)
+        mout[pl.ds(pl.multiple_of(base + HALF, HALF), HALF), :] = lower.astype(BF16)
+
+    step = lax.broadcasted_iota(jnp.int32, (CHUNK, BLOCK), 0)
+    offset = (step % GROUP) * DRAFT + step // GROUP
+
+    def edge_rows():
+        halo_copy().wait_recv()
+        edge = tok[pl.ds(0, HALO), :]
         for b in range(blocks):
-            inner[b] = proj[pl.ds(0, CHUNK), b * BLOCK : (b + 1) * BLOCK].astype(BF16).astype(F32)
-        branch[...] = gelu(proj[pl.ds(0, CHUNK), chans:])
+            columns = w_cat[:, b * BLOCK : (b + 1) * BLOCK]
+            inner_s[b, pl.ds(0, HALO)] = (
+                jnp.dot(edge, columns, preferred_element_type=F32).astype(BF16).astype(F32)
+            )
+
+    def span_chunk(q, following):
+        for b in range(blocks):
+            inner_s[b, pl.ds(pl.multiple_of(HALO + q * CHUNK, HALO), CHUNK)] = (
+                proj[:, b * BLOCK : (b + 1) * BLOCK].astype(BF16).astype(F32)
+            )
+        branch_s[rows_of(q, CHUNK), :] = gelu(proj[:, chans:])
+        position = me * SPAN_ROWS + q * CHUNK + offset
+        begin = jnp.zeros((CHUNK, BLOCK), jnp.int32)
+        for first in firsts:
+            begin = jnp.where(first <= position, first, begin)
+        age = position - begin
+        tokens = token_rows(following)
+        base = HALO - HIST + q * CHUNK
+        for b in range(blocks):
+            project(tokens, b)
+            rows = [
+                inner_s[b, pl.ds(base + i, GROUP, stride=DRAFT), :] for i in range(DRAFT + HIST)
+            ]
+            x = jnp.concatenate(rows, 0)
+            conv = conv_ref[0:1, lanes(b)] * x[HIST * GROUP : HIST * GROUP + CHUNK]
+            for k in range(1, CONV):
+                at = (HIST - k) * GROUP
+                term = conv_ref[k : k + 1, lanes(b)] * x[at : at + CHUNK]
+                conv = conv + jnp.where(age >= k, term, 0.0)
+            decay, drive = gates(conv, b)
+            decay = jnp.where(age > 0, decay, 0.0)
+            h = jnp.zeros((GROUP, BLOCK), F32)
+            a = jnp.ones((GROUP, BLOCK), F32)
+            for t in range(DRAFT):
+                part = slice(t * GROUP, (t + 1) * GROUP)
+                h = decay[part] * h + drive[part]
+                a = decay[part] * a
+                at = pl.ds(pl.multiple_of(q * CHUNK + t * GROUP, GROUP), GROUP)
+                local[at, lanes(b)] = h
+                decays[at, lanes(b)] = a
+            ends_a[rows_of(q, GROUP), lanes(b)] = a
+            ends_h[rows_of(q, GROUP), lanes(b)] = h
+
+    def link(s, carry):
+        product, value = carry
+        at = pl.ds(s, 1)
+        a = ends_a[at, :]
+        h = ends_h[at, :]
+        ends_a[at, :] = product
+        ends_h[at, :] = value
+        return (a * product, a * value + h)
+
+    def send_sums():
+        product, value = lax.fori_loop(
+            0, spans * GROUP, link, (jnp.ones((1, chans), F32), jnp.zeros((1, chans), F32))
+        )
+        sum_send[...] = jnp.zeros_like(sum_send)
+        sum_send[0:1, :] = product
+        sum_send[1:2, :] = value
+        for j in range(1, BACK + 1):
+            sum_copy(j).start()
+
+    def draft_chunk(c, following):
+        for b in range(blocks):
+            inner[b] = proj[:, b * BLOCK : (b + 1) * BLOCK].astype(BF16).astype(F32)
+        branch[...] = gelu(proj[:, chans:])
         members = rows_of(c, GROUP)
         accepted = acc_b[members, :]
-
-        @pl.loop(0, blocks)
-        def _(b):
+        chosen = [accepted == t + 1 for t in range(DRAFT)]
+        tokens = token_rows(following)
+        for b in range(blocks):
+            project(tokens, b)
             rows = [cached_f[j, members, lanes(b)] for j in range(HIST)]
             rows += [inner[b, pl.ds(t, GROUP, stride=DRAFT), :] for t in range(DRAFT)]
             x = jnp.concatenate(rows, 0)
@@ -336,27 +390,65 @@
                 part = slice(t * GROUP, (t + 1) * GROUP)
                 h = decay[part] * h + drive[part]
                 hidden[b, pl.ds(t, GROUP, stride=DRAFT), :] = h
-                chosen = accepted == t + 1
-                picked[0] = jnp.where(chosen, h, picked[0])
+                picked[0] = jnp.where(chosen[t], h, picked[0])
                 for j in range(HIST):
-                    picked[1 + j] = jnp.where(chosen, rows[t + 1 + j], picked[1 + j])
+                    picked[1 + j] = jnp.where(chosen[t], rows[t + 1 + j], picked[1 + j])
             for j in range(1 + HIST):
-                kept[pl.ds(pl.multiple_of(j * requests + c * GROUP, GROUP), GROUP), lanes(b)] = picked[j]
-
-        gated = (branch[...] * spread()).astype(BF16)
-
-        @pl.when(c == 0)
+                at = pl.ds(pl.multiple_of(j * requests + c * GROUP, GROUP), GROUP)
+                kept[at, lanes(b)] = picked[j]
+        project_out(c, (branch[...] * spread()).astype(BF16))
+
+    load_tokens(spans).wait()
+    tokens = token_rows(spans)
+    for n in range(wides):
+        for copy in load_weights(n):
+            copy.wait()
+        project(tokens, n)
+
+    for copy in load_out:
+        copy.start()
+    for q in range(spans):
+        load_tokens(q).start()
+
+    @pl.loop(spans + 1, spans + drafts)
+    def _(i):
+        load_tokens(i).start()
+
+    for copy in small:
+        copy.wait()
+    cached_f[...] = cached[...].astype(F32)
+    rates[0:1, :] = 16.0 * rate_ref[...].reshape(1, chans)
+    for copy in load_out:
+        copy.wait()
+    pl.semaphore_wait(barrier, n_req - 1 + 2)
+    halo_copy().start()
+
+    @pl.loop(0, spans)
+    def _(i):
+        load_tokens(i).wait()
+        draft_chunk(i, i)
+
+        @pl.when(i == 0)
         def _():
-            for copy in loads[6:]:
-                copy.wait()
-            pl.semaphore_wait(barrier, n_req - 1 + 2)
-            halo_copy().start()
-
-        project_out(c, gated)
-
-        @pl.when(c >= lag)
+            edge_rows()
+
+        @pl.when(i >= lag)
         def _():
-            pass_on(c - lag)
+            pass_on(i - lag)
+
+        load_tokens(spans + 1 + i).wait()
+        span_chunk(i, spans + 1 + i)
+
+    send_sums()
+
+    @pl.loop(spans, drafts)
+    def _(c):
+        @pl.when(c < drafts - 1)
+        def _():
+            load_tokens(spans + 1 + c).wait()
+
+        draft_chunk(c, spans + jnp.minimum(c + 1, drafts - 1))
+        pass_on(c - lag)
 
     owner_row = owner_ref[...]
     across = lax.broadcasted_iota(jnp.int32, (requests, requests), 1)
@@ -388,75 +480,10 @@
     local_copy = pltpu.make_async_copy(a2a_send.at[me], a2a_recv.at[me], a2a_send_sem.at[0])
     local_copy.start()
 
-    load_span.wait()
-    halo_copy().wait_recv()
-
-    @pl.loop(0, 2 * chans // (2 * BLOCK))
-    def _(n):
-        at = pl.ds(pl.multiple_of(n * 2 * BLOCK, 2 * BLOCK), 2 * BLOCK)
-        proj[:, at] = jnp.dot(tok_s[...], w_cat[:, at], preferred_element_type=F32)
-
-    for b in range(blocks):
-        inner_s[b] = proj[:, b * BLOCK : (b + 1) * BLOCK].astype(BF16).astype(F32)
-    branch_s[...] = gelu(proj[pl.ds(HALO, SPAN_ROWS), chans:])
-
     @pl.loop(drafts - lag, drafts)
     def _(c):
         pass_on(c)
 
-    step = lax.broadcasted_iota(jnp.int32, (CHUNK, BLOCK), 0)
-    offset = (step % GROUP) * DRAFT + step // GROUP
-
-    @pl.loop(0, spans)
-    def _(q):
-        position = me * SPAN_ROWS + q * CHUNK + offset
-        begin = jnp.zeros((CHUNK, BLOCK), jnp.int32)
-        for first in firsts:
-            begin = jnp.where(first <= position, first, begin)
-        age = position - begin
-
-        @pl.loop(0, blocks)
-        def _(b):
-            base = HALO - HIST + q * CHUNK
-            rows = [
-                inner_s[b, pl.ds(base + i, GROUP, stride=DRAFT), :] for i in range(DRAFT + HIST)
-            ]
-            x = jnp.concatenate(rows, 0)
-            conv = conv_ref[0:1, lanes(b)] * x[HIST * GROUP : HIST * GROUP + CHUNK]
-            for k in range(1, CONV):
-                at = (HIST - k) * GROUP
-                conv = conv + jnp.where(age >= k, conv_ref[k : k + 1, lanes(b)] * x[at : at + CHUNK], 0.0)
-            decay, drive = gates(conv, b)
-            decay = jnp.where(age > 0, decay, 0.0)
-            h = jnp.zeros((GROUP, BLOCK), F32)
-            a = jnp.ones((GROUP, BLOCK), F32)
-            for t in range(DRAFT):
-                part = slice(t * GROUP, (t + 1) * GROUP)
-                h = decay[part] * h + drive[part]
-                a = decay[part] * a
-                at = pl.ds(pl.multiple_of(q * CHUNK + t * GROUP, GROUP), GROUP)
-                local[at, lanes(b)] = h
-                decays[at, lanes(b)] = a
-            ends_a[rows_of(q, GROUP), lanes(b)] = a
-            ends_h[rows_of(q, GROUP), lanes(b)] = h
-
-    def link(s, carry):
-        product, value = carry
-        at = pl.ds(s, 1)
-        a = ends_a[at, :]
-        h = ends_h[at, :]
-        ends_a[at, :] = product
-        ends_h[at, :] = value
-        return (a * product, a * value + h)
-
-    product, value = lax.fori_loop(
-        0, spans * GROUP, link, (jnp.ones((1, chans), F32), jnp.zeros((1, chans), F32))
-    )
-    sum_send[...] = jnp.zeros_like(sum_send)
-    sum_send[0:1, :] = product
-    sum_send[1:2, :] = value
-    for j in range(1, BACK + 1):
-        sum_copy(j).start()
     for j in range(1, BACK + 1):
         sum_copy(j).wait_recv()
     entering = sum_recv[BACK - 1, 1:2, :]
@@ -489,13 +516,6 @@
         oin[j] = (
             got[:, (1 + j) * slots : (2 + j) * slots].astype(F32).reshape(n_req * slots, chans).astype(BF16)
         )
-    ends = [
-        pltpu.make_async_copy(ost, ostate_hbm, end_sem.at[0]),
-        pltpu.make_async_copy(oin, oin_hbm, end_sem.at[1]),
-    ]
-    for copy in ends:
-        copy.start()
-
     @pl.loop(drafts + max(spans - lag, 0), drafts + spans)
     def _(c):
         pass_on(c)
@@ -517,10 +537,6 @@
         for side in range(2):
             first_copy(c, side).wait_send()
             second_copy(c, side).wait_send()
-        out_copy(c).wait()
-
-    for copy in ends:
-        copy.wait()
 
 
 def per_device(
@@ -549,7 +565,7 @@
     drafts = requests * DRAFT // CHUNK
     spans = SPAN_ROWS // CHUNK
     chunks = drafts + spans
-    lag = min(3, spans)
+    lag = min(2, spans)
     vmem, anywhere, smem = (
         pl.BlockSpec(memory_space=pltpu.VMEM),
         pl.BlockSpec(memory_space=pl.ANY),
@@ -559,22 +575,21 @@
     mixed, ostate, oin = pl.pallas_call(
         functools.partial(kernel, lag, n_req, n_ch),
         out_shape=(
-            jax.ShapeDtypeStruct((rows, chans), BF16),
-            jax.ShapeDtypeStruct((n_req * slots, chans), F32),
-            jax.ShapeDtypeStruct((HIST, n_req * slots, chans), BF16),
+            pltpu.VMEM((rows, chans), BF16),
+            pltpu.VMEM((n_req * slots, chans), F32),
+            pltpu.VMEM((HIST, n_req * slots, chans), BF16),
         ),
         in_specs=[smem, vmem, vmem, vmem, vmem] + [anywhere] * 8,
-        out_specs=(anywhere, anywhere, anywhere),
+        out_specs=(vmem, vmem, vmem),
         scratch_shapes=[
             pltpu.VMEM((width, 2 * chans), BF16),
             pltpu.VMEM((chans, n_ch * chans), BF16),
-            pltpu.VMEM((drafts * CHUNK, width), BF16),
-            pltpu.VMEM((HALO + SPAN_ROWS, width), BF16),
+            pltpu.VMEM((HALO + rows, width), BF16),
             pltpu.VMEM((blocks, BLOCK, 2 * BLOCK), BF16),
             pltpu.VMEM((requests, chans), F32),
             pltpu.VMEM((HIST, requests, chans), BF16),
             pltpu.VMEM((HIST, requests, chans), F32),
-            pltpu.VMEM((HALO + SPAN_ROWS, 2 * chans), F32),
+            pltpu.VMEM((CHUNK, 2 * chans), F32),
             pltpu.VMEM((blocks, CHUNK, BLOCK), F32),
             pltpu.VMEM((CHUNK, chans), F32),
             pltpu.VMEM((blocks, CHUNK, BLOCK), F32),
@@ -601,11 +616,10 @@
             pltpu.VMEM((chunks, HALF, chans), BF16),
             pltpu.VMEM((n_req, kinds * slots, chans), BF16),
             pltpu.VMEM((n_req, kinds * slots, chans), BF16),
-            pltpu.VMEM((rows, chans), BF16),
-            pltpu.VMEM((n_req * slots, chans), F32),
-            pltpu.VMEM((HIST, n_req * slots, chans), BF16),
-            dma((11,)),
-            dma((drafts,)),
+            pltpu.VMEM((8, chans), F32),
+            dma((9,)),
+            dma((2 * chans // WIDE, 2)),
+            dma((chunks,)),
             dma,
             dma,
             dma((BACK,)),
@@ -616,11 +630,9 @@
             dma((chunks, 2)),
             dma((n_req,)),
             dma((n_req,)),
-            dma((chunks,)),
-            dma((2,)),
         ],
         compiler_params=pltpu.CompilerParams(
-            collective_id=0, has_side_effects=True, vmem_limit_bytes=60 * 1024 * 1024
+            collective_id=0, has_side_effects=True, vmem_limit_bytes=52 * 1024 * 1024
         ),
         name="griffin",
     )(
@@ -628,7 +640,7 @@
         accepted.reshape(1, requests),
         owner.reshape(1, requests),
         conv_w,
-        decay_rate.reshape(1, chans),
+        decay_rate,
         tokens,
         w_in,
         w_gate,

time: 93.5 us -> 85.9 us (0.919)
  the two profiles are of different devices: /device:TPU:1 before, /device:TPU:6 now
where the time goes in v1:
time: 85.9 us; the launch traced here: 84.9 us
  Pallas kernels  81.5 us (95%)
  local copies, waits for them, and re-layouts  2.78 us (3%)
    pallas_call x1, Pallas kernels, per_device(): pl.pallas_call(functools.partial(kernel, lag, n_req, n_ch), out_shape=(pl...  81.5 us
    unnamed x3, local copies, waits for them, and re-layouts  2.78 us

profile of v1, /device:TPU:6, one launch (start us, length us, event | category | flops | bytes accessed | tf_op | source)
XLA Modules:
  0.0 84.9 jit_solution(512824932397807294)
XLA Ops:
  0.6 81.5 %griffin.1 = (bf16[1536,640]{1,0:T(8,128)(2,1)S(1)}, f32[128,640]{1,0:T(8,128)S(1)}, bf16[3,128,640]{2,1,0:T(8,128)(2,1)S(1)}) custom-call(s32[16]{0:T(128)} %span_ref.1, s32[1,64]{1,0:T(1,128)} %bitcast.10, s32[1,64]{1,0:T(1,128)} %bitcast.11, f32[4,640]{1,0:T(4,128)} %conv_ref.1, f32[640]{0:T(1024)} %rate_ref.1, bf16[1536,2560]{1,0:T(8,128)(2,1)} %tokens_hbm.1, ...), custom_call_target="tpu_custom_call" | custom-call | tf_op jit(solution)/shard_map/griffin/pallas_call | solution.py:575
  82.1 1.3 %copy.19 = bf16[1536,640]{1,0:T(8,128)(2,1)} copy(bf16[1536,640]{1,0:T(8,128)(2,1)S(1)} %get-tuple-element.9) | data formatting | bytes 3932160
  83.4 0.7 copy.20
  84.1 0.8 copy.21

commit v2 on v1

--- a/solution.py
+++ b/solution.py
@@ -260,7 +260,7 @@
     def spread():
         return jnp.concatenate([hidden[b] for b in range(blocks)], 1)
 
-    def project_out(c, gated):
+    def project_out(c, gated, opening=False):
         def shares(k):
             at = slice(k * chans, (k + 2) * chans)
             both = jnp.dot(gated, w_out[:, at], preferred_element_type=F32)
@@ -271,12 +271,16 @@
         send_l[c, pl.ds(0, HALF)] = to_far[HALF:]
         stash_r[c] = to_right[:HALF]
         send_r[c, pl.ds(HALF, HALF)] = to_right[HALF:]
+        if opening:
+            pl.semaphore_wait(barrier, n_req - 1 + 2)
         first_copy(c, 0).start()
         to_left, to_own = shares(2)
         send_l[c, pl.ds(HALF, HALF)] = to_left[:HALF]
         stash_l[c] = to_left[HALF:]
         first_copy(c, 1).start()
         own[c] = to_own
+        if opening:
+            halo_copy().start()
 
     def pass_on(c):
         first_copy(c, 0).wait_recv()
@@ -366,7 +370,7 @@
         for j in range(1, BACK + 1):
             sum_copy(j).start()
 
-    def draft_chunk(c, following):
+    def draft_chunk(c, following, opening=False):
         for b in range(blocks):
             inner[b] = proj[:, b * BLOCK : (b + 1) * BLOCK].astype(BF16).astype(F32)
         branch[...] = gelu(proj[:, chans:])
@@ -396,7 +400,7 @@
             for j in range(1 + HIST):
                 at = pl.ds(pl.multiple_of(j * requests + c * GROUP, GROUP), GROUP)
                 kept[at, lanes(b)] = picked[j]
-        project_out(c, (branch[...] * spread()).astype(BF16))
+        project_out(c, (branch[...] * spread()).astype(BF16), opening)
 
     load_tokens(spans).wait()
     tokens = token_rows(spans)
@@ -420,28 +424,28 @@
     rates[0:1, :] = 16.0 * rate_ref[...].reshape(1, chans)
     for copy in load_out:
         copy.wait()
-    pl.semaphore_wait(barrier, n_req - 1 + 2)
-    halo_copy().start()
+    load_tokens(spans + 1).wait()
+    draft_chunk(0, spans + 1, opening=True)
 
     @pl.loop(0, spans)
     def _(i):
         load_tokens(i).wait()
-        draft_chunk(i, i)
+        draft_chunk(i + 1, i)
 
         @pl.when(i == 0)
         def _():
             edge_rows()
 
-        @pl.when(i >= lag)
+        @pl.when(i > 0)
         def _():
-            pass_on(i - lag)
-
-        load_tokens(spans + 1 + i).wait()
-        span_chunk(i, spans + 1 + i)
+            pass_on(i - 1)
+
+        load_tokens(spans + 2 + i).wait()
+        span_chunk(i, spans + 2 + i)
 
     send_sums()
 
-    @pl.loop(spans, drafts)
+    @pl.loop(spans + 1, drafts)
     def _(c):
         @pl.when(c < drafts - 1)
         def _():
@@ -537,6 +541,18 @@
         for side in range(2):
             first_copy(c, side).wait_send()
             second_copy(c, side).wait_send()
+
+
+def write_out(*refs):
+    sources, targets, sems = refs[:3], refs[3:6], refs[6]
+    copies = [
+        pltpu.make_async_copy(source, target, sems.at[i])
+        for i, (source, target) in enumerate(zip(sources, targets))
+    ]
+    for copy in copies:
+        copy.start()
+    for copy in copies:
+        copy.wait()
 
 
 def per_device(
@@ -650,6 +666,14 @@
         cached_state,
         jnp.transpose(cached_inputs, (1, 0, 2)),
     )
+    mixed, ostate, oin = pl.pallas_call(
+        write_out,
+        out_shape=tuple(jax.ShapeDtypeStruct(a.shape, a.dtype) for a in (mixed, ostate, oin)),
+        in_specs=[vmem] * 3,
+        out_specs=(anywhere,) * 3,
+        scratch_shapes=[dma((3,))],
+        name="write_out",
+    )(*(pltpu.with_memory_space_constraint(a, pltpu.VMEM) for a in (mixed, ostate, oin)))
     return (
         mixed,
         ostate.reshape(1, n_req * slots, chans),

time: 85.9 us -> 83.2 us (0.969)
  local copies, waits for them, and re-layouts: 2.78 us -> 0 us
    unnamed x3 -> x0, local copies, waits for them, and re-layouts: 2.78 us -> none
    pallas_call x0 -> x1, Pallas kernels: none -> 1.56 us  [per_device(): pl.pallas_call(write_out, out_shape=tuple((jax.ShapeDtypeStruct(a.shape,...]
    pallas_call x1, Pallas kernels: 81.5 us -> 80.2 us  [per_device(): pl.pallas_call(functools.partial(kernel, lag, n_req, n_ch), out_shape=(pl...]
where the time goes in v2:
time: 83.2 us; the launch traced here: 82.4 us
  Pallas kernels  81.8 us (98%)
    pallas_call x1, Pallas kernels, per_device(): pl.pallas_call(functools.partial(kernel, lag, n_req, n_ch), out_shape=(pl...  80.2 us

profile of v2, /device:TPU:6, one launch (start us, length us, event | category | flops | bytes accessed | tf_op | source)
XLA Modules:
  0.0 82.4 jit_solution(9180452868476707731)
XLA Ops:
  0.6 80.2 %griffin.1 = (bf16[1536,640]{1,0:T(8,128)(2,1)S(1)}, f32[128,640]{1,0:T(8,128)S(1)}, bf16[3,128,640]{2,1,0:T(8,128)(2,1)S(1)}) custom-call(s32[16]{0:T(128)} %span_ref.1, s32[1,64]{1,0:T(1,128)} %bitcast.8, s32[1,64]{1,0:T(1,128)} %bitcast.9, f32[4,640]{1,0:T(4,128)} %conv_ref.1, f32[640]{0:T(1024)} %rate_ref.1, bf16[1536,2560]{1,0:T(8,128)(2,1)} %tokens_hbm.1, ...), custom_call_target="tpu_custom_call" | custom-call | tf_op jit(solution)/shard_map/griffin/pallas_call | solution.py:591
  80.9 1.6 %write_out.1 = (bf16[1536,640]{1,0:T(8,128)(2,1)}, f32[128,640]{1,0:T(8,128)}, bf16[3,128,640]{2,1,0:T(8,128)(2,1)}) custom-call(bf16[1536,640]{1,0:T(8,128)(2,1)S(1)} %get-tuple-element.9.refs_0_, f32[128,640]{1,0:T(8,128)S(1)} %get-tuple-element.10.refs_1_, bf16[3,128,640]{2,1,0:T(8,128)(2,1)S(1)} %get-tuple-element.11.refs_2_), custom_call_target="tpu_custom_call" | custom-call | tf_op jit(solution)/shard_map/write_out/pallas_call | solution.py:669

commit v3 on v2

--- a/solution.py
+++ b/solution.py
@@ -18,6 +18,7 @@
 GROUP = CHUNK // DRAFT
 HALO = 16
 BACK = 4
+RING = 6
 MESH = pl.DeviceIdType.MESH
 F32 = jnp.float32
 BF16 = jnp.bfloat16
@@ -74,16 +75,23 @@
     sum_send,
     sum_recv,
     own,
-    stash_r,
-    stash_l,
-    send_r,
-    send_l,
-    recv_l,
-    recv_r,
-    send2_r,
-    send2_l,
-    recv2_l,
-    recv2_r,
+    stash_p,
+    stash_q,
+    send_p,
+    send_q,
+    recv_p,
+    recv_q,
+    send2_p,
+    send2_q,
+    recv2_p,
+    recv2_q,
+    gated_x,
+    gated_r,
+    pair_send,
+    pair_recv,
+    pair_own,
+    last_send,
+    last_recv,
     a2a_send,
     a2a_recv,
     rates,
@@ -100,6 +108,13 @@
     two_recv,
     a2a_send_sem,
     a2a_recv_sem,
+    piece_sem,
+    spread_send,
+    spread_recv,
+    core_send,
+    core_recv,
+    pair_send_sem,
+    pair_recv_sem,
 ):
     chans = w_in_hbm.shape[1]
     blocks = chans // BLOCK
@@ -110,12 +125,27 @@
     wides = 2 * chans // WIDE
     me = lax.axis_index("req")
     place = lax.axis_index("ch")
-    right = lax.rem(place + 1, n_ch)
-    left = lax.rem(place + n_ch - 1, n_ch)
+    odd = lax.rem(place, 2)
+    mate = place + 1 - 2 * odd
+    other = lax.rem(place + n_ch - 1 + 2 * odd, n_ch)
     far = lax.rem(place + 2, n_ch)
+    mine = lax.rem((place + 1) // 2, 2)
+    groups = n_req // n_ch
+    piece_rows = chans // groups
+    kind = me // groups
+    piece = lax.rem(me, groups)
 
     def peer(j):
         return lax.rem(me + j, n_req)
+
+    barrier = pltpu.get_barrier_semaphore()
+
+    @pl.loop(1, n_req)
+    def _(j):
+        pl.semaphore_signal(barrier, inc=1, device_id={"req": peer(j)}, device_id_type=MESH)
+
+    for side in (mate, other):
+        pl.semaphore_signal(barrier, inc=1, device_id={"ch": side}, device_id_type=MESH)
 
     def load_weights(n):
         pieces = []
@@ -138,11 +168,11 @@
         pltpu.make_async_copy(cached_hbm, cached, load_sem.at[3]),
     ]
     load_out = []
-    for k, source in enumerate((far, right, left, place)):
+    for k, source in enumerate((far, other, place, mate)):
         columns = pl.ds(pl.multiple_of(source * chans, BLOCK), chans)
         load_out.append(
             pltpu.make_async_copy(
-                w_out_hbm.at[:, columns], w_out.at[:, pl.ds(k * chans, chans)], load_sem.at[4 + k]
+                w_out_hbm.at[:, columns], w_out.at[pl.ds(0, chans), pl.ds(k * chans, chans)], load_sem.at[4 + k]
             )
         )
 
@@ -162,15 +192,6 @@
             copy.start()
     for copy in small:
         copy.start()
-
-    barrier = pltpu.get_barrier_semaphore()
-
-    @pl.loop(1, n_req)
-    def _(j):
-        pl.semaphore_signal(barrier, inc=1, device_id={"req": peer(j)}, device_id_type=MESH)
-
-    for side in (left, right):
-        pl.semaphore_signal(barrier, inc=1, device_id={"ch": side}, device_id_type=MESH)
 
     def halo_copy():
         return pltpu.make_async_remote_copy(
@@ -183,7 +204,7 @@
         )
 
     def first_copy(c, side):
-        source, target, device = ((send_r, recv_l, right), (send_l, recv_r, left))[side]
+        source, target, device = ((send_p, recv_p, mate), (send_q, recv_q, other))[side]
         return pltpu.make_async_remote_copy(
             src_ref=source.at[c],
             dst_ref=target.at[c],
@@ -194,7 +215,7 @@
         )
 
     def second_copy(c, side):
-        source, target, device = ((send2_r, recv2_l, right), (send2_l, recv2_r, left))[side]
+        source, target, device = ((send2_p, recv2_p, mate), (send2_q, recv2_q, other))[side]
         return pltpu.make_async_remote_copy(
             src_ref=source.at[c],
             dst_ref=target.at[c],
@@ -263,41 +284,143 @@
     def project_out(c, gated, opening=False):
         def shares(k):
             at = slice(k * chans, (k + 2) * chans)
-            both = jnp.dot(gated, w_out[:, at], preferred_element_type=F32)
+            both = jnp.dot(gated, w_out[pl.ds(0, chans), at], preferred_element_type=F32)
             return both[:, :chans].astype(BF16), both[:, chans:].astype(BF16)
 
-        to_far, to_right = shares(0)
-        send_r[c, pl.ds(0, HALF)] = to_far[:HALF]
-        send_l[c, pl.ds(0, HALF)] = to_far[HALF:]
-        stash_r[c] = to_right[:HALF]
-        send_r[c, pl.ds(HALF, HALF)] = to_right[HALF:]
+        to_far, to_other = shares(0)
+        send_p[c, pl.ds(0, HALF)] = to_far[:HALF]
+        send_q[c, pl.ds(0, HALF)] = to_far[HALF:]
+        stash_q[c] = to_other[:HALF]
+        send_q[c, pl.ds(HALF, HALF)] = to_other[HALF:]
         if opening:
             pl.semaphore_wait(barrier, n_req - 1 + 2)
+            halo_copy().start()
+            piece_copy().start()
+        first_copy(c, 1).start()
+        to_own, to_mate = shares(2)
+        send_p[c, pl.ds(HALF, HALF)] = to_mate[:HALF]
+        stash_p[c] = to_mate[HALF:]
         first_copy(c, 0).start()
-        to_left, to_own = shares(2)
-        send_l[c, pl.ds(HALF, HALF)] = to_left[:HALF]
-        stash_l[c] = to_left[HALF:]
-        first_copy(c, 1).start()
         own[c] = to_own
-        if opening:
-            halo_copy().start()
 
     def pass_on(c):
         first_copy(c, 0).wait_recv()
-        send2_r[c] = (recv_l[c, pl.ds(0, HALF)].astype(F32) + stash_r[c].astype(F32)).astype(BF16)
+        send2_q[c] = (recv_p[c, pl.ds(0, HALF)].astype(F32) + stash_q[c].astype(F32)).astype(BF16)
+        second_copy(c, 1).start()
+        first_copy(c, 1).wait_recv()
+        send2_p[c] = (recv_q[c, pl.ds(0, HALF)].astype(F32) + stash_p[c].astype(F32)).astype(BF16)
         second_copy(c, 0).start()
-        first_copy(c, 1).wait_recv()
-        send2_l[c] = (recv_r[c, pl.ds(0, HALF)].astype(F32) + stash_l[c].astype(F32)).astype(BF16)
-        second_copy(c, 1).start()
+
+    def slot_of_kind(device):
+        step = lax.rem(kind - device + n_ch, n_ch)
+        parity = lax.rem(device, 2)
+        turned = lax.rem(step + parity * (n_ch - 2 * step) + n_ch, n_ch)
+        return pl.multiple_of(lax.rem(turned + 2, n_ch) * chans, BLOCK)
+
+    def piece_copy():
+        rows = pl.multiple_of(piece * piece_rows, 16)
+        columns = pl.multiple_of(kind * chans, BLOCK)
+        return pltpu.make_async_remote_copy(
+            src_ref=w_out_hbm.at[pl.ds(rows, piece_rows), pl.ds(columns, chans)],
+            dst_ref=w_out.at[pl.ds(pl.multiple_of(chans + rows, 16), piece_rows), pl.ds(slot_of_kind(mate), chans)],
+            send_sem=piece_sem.at[0],
+            recv_sem=piece_sem.at[1],
+            device_id={"ch": mate},
+            device_id_type=MESH,
+        )
+
+    def spread_copy(j):
+        rows = pl.multiple_of(chans + piece * piece_rows, 16)
+        part = w_out.at[pl.ds(rows, piece_rows), pl.ds(slot_of_kind(place), chans)]
+        return pltpu.make_async_remote_copy(
+            src_ref=part,
+            dst_ref=part,
+            send_sem=spread_send.at[j],
+            recv_sem=spread_recv.at[j],
+            device_id={"req": peer(2 * j)},
+            device_id_type=MESH,
+        )
+
+    def core_copy(g):
+        rows = pl.multiple_of(chans + (2 * g + lax.rem(me, 2)) * piece_rows, 16)
+        part = w_out.at[pl.ds(rows, piece_rows)]
+        return pltpu.make_async_remote_copy(
+            src_ref=part,
+            dst_ref=part,
+            send_sem=core_send.at[g],
+            recv_sem=core_recv.at[g],
+            device_id={"req": me + 1 - 2 * lax.rem(me, 2)},
+            device_id_type=MESH,
+        )
+
+    def spread_pieces():
+        piece_copy().wait_recv()
+
+        @pl.loop(1, n_req // 2)
+        def _(j):
+            spread_copy(j).start()
+
+    def swap_cores():
+        @pl.loop(1, n_req // 2)
+        def _(j):
+            spread_copy(j).wait_recv()
+
+        for g in range(groups // 2):
+            core_copy(g).start()
+
+    def pair_copy(stage, j):
+        source, target, device = (
+            (gated_x.at[j, 1 - mine], gated_r.at[j], mate),
+            (pair_send.at[0, j], pair_recv.at[0, j], other),
+            (pair_send.at[1, j], pair_recv.at[1, j], other),
+            (last_send.at[j], last_recv.at[j], mate),
+        )[stage]
+        return pltpu.make_async_remote_copy(
+            src_ref=source,
+            dst_ref=target,
+            send_sem=pair_send_sem.at[stage, j],
+            recv_sem=pair_recv_sem.at[stage, j],
+            device_id={"ch": device},
+            device_id_type=MESH,
+        )
+
+    def pair_project(j):
+        pair_copy(0, j).wait_recv()
+        both = jnp.concatenate([gated_x[j, mine], gated_r[j]], 1)
+        outer = jnp.dot(both, w_out[:, : 2 * chans], preferred_element_type=F32)
+        pair_send[0, j] = outer[:, :chans].astype(BF16)
+        pair_copy(1, j).start()
+        pair_send[1, j] = outer[:, chans:].astype(BF16)
+        pair_copy(2, j).start()
+        pair_own[j] = jnp.dot(both, w_out[:, 2 * chans :], preferred_element_type=F32)
+
+    def pair_rows(j, chunk):
+        first = RING + 2 * j
+        base = jnp.where(first < drafts, SPAN_ROWS + first * CHUNK, (first - drafts) * CHUNK)
+        return pl.ds(pl.multiple_of(base + chunk * CHUNK, CHUNK), CHUNK)
+
+    def pair_sum(j):
+        pair_copy(1, j).wait_recv()
+        last_send[j] = (pair_own[j, :, chans:] + pair_recv[0, j].astype(F32)).astype(BF16)
+        pair_copy(3, j).start()
+
+    def pair_keep(j):
+        pair_copy(2, j).wait_recv()
+        total = pair_own[j, :, :chans] + pair_recv[1, j].astype(F32)
+        mout[pair_rows(j, mine), :] = total.astype(BF16)
+
+    def pair_finish(j):
+        pair_copy(3, j).wait_recv()
+        mout[pair_rows(j, 1 - mine), :] = last_recv[j]
 
     def finish(c):
         second_copy(c, 0).wait_recv()
         second_copy(c, 1).wait_recv()
-        upper = own[c, pl.ds(0, HALF)].astype(F32) + recv2_l[c].astype(F32)
-        lower = own[c, pl.ds(HALF, HALF)].astype(F32) + recv2_r[c].astype(F32)
-        upper = upper + recv_r[c, pl.ds(HALF, HALF)].astype(F32)
-        lower = lower + recv_l[c, pl.ds(HALF, HALF)].astype(F32)
-        base = jnp.where(c < drafts, SPAN_ROWS + c * CHUNK, (c - drafts) * CHUNK)
+        upper = own[c, pl.ds(0, HALF)].astype(F32) + recv2_q[c].astype(F32)
+        lower = own[c, pl.ds(HALF, HALF)].astype(F32) + recv2_p[c].astype(F32)
+        upper = upper + recv_p[c, pl.ds(HALF, HALF)].astype(F32)
+        lower = lower + recv_q[c, pl.ds(HALF, HALF)].astype(F32)
+        base = SPAN_ROWS + c * CHUNK
         mout[pl.ds(pl.multiple_of(base, HALF), HALF), :] = upper.astype(BF16)
         mout[pl.ds(pl.multiple_of(base + HALF, HALF), HALF), :] = lower.astype(BF16)
 
@@ -370,7 +493,7 @@
         for j in range(1, BACK + 1):
             sum_copy(j).start()
 
-    def draft_chunk(c, following, opening=False):
+    def draft_chunk(c, following):
         for b in range(blocks):
             inner[b] = proj[:, b * BLOCK : (b + 1) * BLOCK].astype(BF16).astype(F32)
         branch[...] = gelu(proj[:, chans:])
@@ -400,7 +523,7 @@
             for j in range(1 + HIST):
                 at = pl.ds(pl.multiple_of(j * requests + c * GROUP, GROUP), GROUP)
                 kept[at, lanes(b)] = picked[j]
-        project_out(c, (branch[...] * spread()).astype(BF16), opening)
+        return (branch[...] * spread()).astype(BF16)
 
     load_tokens(spans).wait()
     tokens = token_rows(spans)
@@ -425,16 +548,17 @@
     for copy in load_out:
         copy.wait()
     load_tokens(spans + 1).wait()
-    draft_chunk(0, spans + 1, opening=True)
+    project_out(0, draft_chunk(0, spans + 1), opening=True)
 
     @pl.loop(0, spans)
     def _(i):
         load_tokens(i).wait()
-        draft_chunk(i + 1, i)
+        project_out(i + 1, draft_chunk(i + 1, i))
 
         @pl.when(i == 0)
         def _():
             edge_rows()
+            spread_pieces()
 
         @pl.when(i > 0)
         def _():
@@ -445,14 +569,54 @@
 
     send_sums()
 
-    @pl.loop(spans + 1, drafts)
-    def _(c):
+    def draft_step(c):
         @pl.when(c < drafts - 1)
         def _():
             load_tokens(spans + 1 + c).wait()
 
-        draft_chunk(c, spans + jnp.minimum(c + 1, drafts - 1))
+        return draft_chunk(c, spans + jnp.minimum(c + 1, drafts - 1))
+
+    @pl.loop(spans + 1, RING)
+    def _(c):
+        project_out(c, draft_step(c))
         pass_on(c - lag)
+
+    for j in range(1, BACK + 1):
+        sum_copy(j).wait_recv()
+    entering = sum_recv[BACK - 1, 1:2, :]
+    for j in range(BACK - 2, -1, -1):
+        entering = sum_recv[j, 0:1, :] * entering + sum_recv[j, 1:2, :]
+
+    @pl.loop(0, spans)
+    def _(q):
+        carry = ends_h[rows_of(q, GROUP), :] + ends_a[rows_of(q, GROUP), :] * entering
+        for t in range(DRAFT):
+            at = pl.ds(pl.multiple_of(q * CHUNK + t * GROUP, GROUP), GROUP)
+            h = local[at, :] + decays[at, :] * carry
+            for b in range(blocks):
+                hidden[b, pl.ds(t, GROUP, stride=DRAFT), :] = h[:, b * BLOCK : (b + 1) * BLOCK]
+        gated_x[1 + q // 2, lax.rem(q, 2)] = (branch_s[rows_of(q, CHUNK), :] * spread()).astype(BF16)
+
+        @pl.when(lax.rem(q, 2) == 1)
+        def _():
+            pair_copy(0, 1 + q // 2).start()
+
+    swap_cores()
+
+    @pl.loop(RING, drafts)
+    def _(c):
+        gated_x[0, c - RING] = draft_step(c)
+        pass_on(c - lag)
+
+    pair_copy(0, 0).start()
+
+    for g in range(groups // 2):
+        core_copy(g).wait_recv()
+    pairs = (drafts + spans - RING) // 2
+
+    @pl.loop(0, pairs)
+    def _(j):
+        pair_project(lax.rem(j + 1, pairs))
 
     owner_row = owner_ref[...]
     across = lax.broadcasted_iota(jnp.int32, (requests, requests), 1)
@@ -484,29 +648,16 @@
     local_copy = pltpu.make_async_copy(a2a_send.at[me], a2a_recv.at[me], a2a_send_sem.at[0])
     local_copy.start()
 
-    @pl.loop(drafts - lag, drafts)
+    pair_sum(1)
+    pair_keep(1)
+    pair_sum(2)
+
+    @pl.loop(0, RING)
     def _(c):
-        pass_on(c)
-
-    for j in range(1, BACK + 1):
-        sum_copy(j).wait_recv()
-    entering = sum_recv[BACK - 1, 1:2, :]
-    for j in range(BACK - 2, -1, -1):
-        entering = sum_recv[j, 0:1, :] * entering + sum_recv[j, 1:2, :]
-
-    @pl.loop(0, spans)
-    def _(q):
-        carry = ends_h[rows_of(q, GROUP), :] + ends_a[rows_of(q, GROUP), :] * entering
-        for t in range(DRAFT):
-            at = pl.ds(pl.multiple_of(q * CHUNK + t * GROUP, GROUP), GROUP)
-            h = local[at, :] + decays[at, :] * carry
-            for b in range(blocks):
-                hidden[b, pl.ds(t, GROUP, stride=DRAFT), :] = h[:, b * BLOCK : (b + 1) * BLOCK]
-        project_out(drafts + q, (branch_s[rows_of(q, CHUNK), :] * spread()).astype(BF16))
-
-        @pl.when(q >= lag)
-        def _():
-            pass_on(drafts + q - lag)
+        finish(c)
+
+    pair_keep(2)
+    pair_sum(0)
 
     local_copy.wait()
 
@@ -520,15 +671,25 @@
         oin[j] = (
             got[:, (1 + j) * slots : (2 + j) * slots].astype(F32).reshape(n_req * slots, chans).astype(BF16)
         )
-    @pl.loop(drafts + max(spans - lag, 0), drafts + spans)
-    def _(c):
-        pass_on(c)
-
-    @pl.loop(0, drafts + spans)
-    def _(c):
-        finish(c)
+    pair_keep(0)
+    for j in (1, 2, 0):
+        pair_finish(j)
 
     halo_copy().wait_send()
+    piece_copy().wait_send()
+
+    @pl.loop(1, n_req // 2)
+    def _(j):
+        spread_copy(j).wait_send()
+
+    for g in range(groups // 2):
+        core_copy(g).wait_send()
+
+    @pl.loop(0, pairs)
+    def _(j):
+        for stage in range(4):
+            pair_copy(stage, j).wait_send()
+
     for j in range(1, BACK + 1):
         sum_copy(j).wait_send()
 
@@ -536,7 +697,7 @@
     def _(j):
         a2a_copy(j).wait_send()
 
-    @pl.loop(0, drafts + spans)
+    @pl.loop(0, RING)
     def _(c):
         for side in range(2):
             first_copy(c, side).wait_send()
@@ -581,6 +742,7 @@
     drafts = requests * DRAFT // CHUNK
     spans = SPAN_ROWS // CHUNK
     chunks = drafts + spans
+    pairs = (chunks - RING) // 2
     lag = min(2, spans)
     vmem, anywhere, smem = (
         pl.BlockSpec(memory_space=pltpu.VMEM),
@@ -599,7 +761,7 @@
         out_specs=(vmem, vmem, vmem),
         scratch_shapes=[
             pltpu.VMEM((width, 2 * chans), BF16),
-            pltpu.VMEM((chans, n_ch * chans), BF16),
+            pltpu.VMEM((2 * chans, n_ch * chans), BF16),
             pltpu.VMEM((HALO + rows, width), BF16),
             pltpu.VMEM((blocks, BLOCK, 2 * BLOCK), BF16),
             pltpu.VMEM((requests, chans), F32),
@@ -619,17 +781,24 @@
             pltpu.VMEM((spans * GROUP, chans), F32),
             pltpu.VMEM((8, chans), F32),
             pltpu.VMEM((BACK, 8, chans), F32),
-            pltpu.VMEM((chunks, CHUNK, chans), BF16),
-            pltpu.VMEM((chunks, HALF, chans), BF16),
-            pltpu.VMEM((chunks, HALF, chans), BF16),
-            pltpu.VMEM((chunks, CHUNK, chans), BF16),
-            pltpu.VMEM((chunks, CHUNK, chans), BF16),
-            pltpu.VMEM((chunks, CHUNK, chans), BF16),
-            pltpu.VMEM((chunks, CHUNK, chans), BF16),
-            pltpu.VMEM((chunks, HALF, chans), BF16),
-            pltpu.VMEM((chunks, HALF, chans), BF16),
-            pltpu.VMEM((chunks, HALF, chans), BF16),
-            pltpu.VMEM((chunks, HALF, chans), BF16),
+            pltpu.VMEM((RING, CHUNK, chans), BF16),
+            pltpu.VMEM((RING, HALF, chans), BF16),
+            pltpu.VMEM((RING, HALF, chans), BF16),
+            pltpu.VMEM((RING, CHUNK, chans), BF16),
+            pltpu.VMEM((RING, CHUNK, chans), BF16),
+            pltpu.VMEM((RING, CHUNK, chans), BF16),
+            pltpu.VMEM((RING, CHUNK, chans), BF16),
+            pltpu.VMEM((RING, HALF, chans), BF16),
+            pltpu.VMEM((RING, HALF, chans), BF16),
+            pltpu.VMEM((RING, HALF, chans), BF16),
+            pltpu.VMEM((RING, HALF, chans), BF16),
+            pltpu.VMEM((pairs, 2, CHUNK, chans), BF16),
+            pltpu.VMEM((pairs, CHUNK, chans), BF16),
+            pltpu.VMEM((2, pairs, CHUNK, chans), BF16),
+            pltpu.VMEM((2, pairs, CHUNK, chans), BF16),
+            pltpu.VMEM((pairs, CHUNK, 2 * chans), F32),
+            pltpu.VMEM((pairs, CHUNK, chans), BF16),
+            pltpu.VMEM((pairs, CHUNK, chans), BF16),
             pltpu.VMEM((n_req, kinds * slots, chans), BF16),
             pltpu.VMEM((n_req, kinds * slots, chans), BF16),
             pltpu.VMEM((8, chans), F32),
@@ -640,12 +809,19 @@
             dma,
             dma((BACK,)),
             dma((BACK,)),
-            dma((chunks, 2)),
-            dma((chunks, 2)),
-            dma((chunks, 2)),
-            dma((chunks, 2)),
+            dma((RING, 2)),
+            dma((RING, 2)),
+            dma((RING, 2)),
+            dma((RING, 2)),
             dma((n_req,)),
             dma((n_req,)),
+            dma((2,)),
+            dma((n_req // 2,)),
+            dma((n_req // 2,)),
+            dma((n_req // n_ch // 2,)),
+            dma((n_req // n_ch // 2,)),
+            dma((4, pairs)),
+            dma((4, pairs)),
         ],
         compiler_params=pltpu.CompilerParams(
             collective_id=0, has_side_effects=True, vmem_limit_bytes=52 * 1024 * 1024

time: 83.2 us -> 80.9 us (0.972)
  Pallas kernels: 81.8 us -> 80.1 us
    pallas_call x1, Pallas kernels: 80.2 us -> 78.5 us  [per_device(): pl.pallas_call(functools.partial(kernel, lag, n_req, n_ch), out_shape=(pl...]
where the time goes in v3:
time: 80.9 us; the launch traced here: 80.7 us
  Pallas kernels  80.1 us (99%)
    pallas_call x1, Pallas kernels, per_device(): pl.pallas_call(functools.partial(kernel, lag, n_req, n_ch), out_shape=(pl...  78.5 us

profile of v3, /device:TPU:6, one launch (start us, length us, event | category | flops | bytes accessed | tf_op | source)
XLA Modules:
  0.0 80.7 jit_solution(1098929244108625731)
XLA Ops:
  0.6 78.5 %griffin.1 = (bf16[1536,640]{1,0:T(8,128)(2,1)S(1)}, f32[128,640]{1,0:T(8,128)S(1)}, bf16[3,128,640]{2,1,0:T(8,128)(2,1)S(1)}) custom-call(s32[16]{0:T(128)} %span_ref.1, s32[1,64]{1,0:T(1,128)} %bitcast.8, s32[1,64]{1,0:T(1,128)} %bitcast.9, f32[4,640]{1,0:T(4,128)} %conv_ref.1, f32[640]{0:T(1024)} %rate_ref.1, bf16[1536,2560]{1,0:T(8,128)(2,1)} %tokens_hbm.1, ...), custom_call_target="tpu_custom_call" | custom-call | tf_op jit(solution)/shard_map/griffin/pallas_call | solution.py:753
  79.1 1.6 %write_out.1 = (bf16[1536,640]{1,0:T(8,128)(2,1)}, f32[128,640]{1,0:T(8,128)}, bf16[3,128,640]{2,1,0:T(8,128)(2,1)}) custom-call(bf16[1536,640]{1,0:T(8,128)(2,1)S(1)} %get-tuple-element.9.refs_0_, f32[128,640]{1,0:T(8,128)S(1)} %get-tuple-element.10.refs_1_, bf16[3,128,640]{2,1,0:T(8,128)(2,1)S(1)} %get-tuple-element.11.refs_2_), custom_call_target="tpu_custom_call" | custom-call | tf_op jit(solution)/shard_map/write_out/pallas_call | solution.py:845

commit v4 on v3

--- a/solution.py
+++ b/solution.py
@@ -360,13 +360,16 @@
         def _(j):
             spread_copy(j).start()
 
-    def swap_cores():
-        @pl.loop(1, n_req // 2)
-        def _(j):
-            spread_copy(j).wait_recv()
-
-        for g in range(groups // 2):
-            core_copy(g).start()
+    def swap_cores(g):
+        for k in range(n_ch):
+            source = k * groups + 2 * g + lax.rem(me, 2)
+            j = lax.rem(me - source + n_req, n_req) // 2
+
+            @pl.when(j > 0)
+            def _():
+                spread_copy(j).wait_recv()
+
+        core_copy(g).start()
 
     def pair_copy(stage, j):
         source, target, device = (
@@ -601,7 +604,8 @@
         def _():
             pair_copy(0, 1 + q // 2).start()
 
-    swap_cores()
+    for g in range(groups // 2):
+        swap_cores(g)
 
     @pl.loop(RING, drafts)
     def _(c):

time: 80.9 us -> 80.9 us (level)
  no operation moved by 1% of the time
where the time goes in v4:
time: 80.9 us; the launch traced here: 80.7 us
  Pallas kernels  80.1 us (99%)
    pallas_call x1, Pallas kernels, per_device(): pl.pallas_call(functools.partial(kernel, lag, n_req, n_ch), out_shape=(pl...  78.5 us

profile of v4, /device:TPU:6, one launch (start us, length us, event | category | flops | bytes accessed | tf_op | source)
XLA Modules:
  0.0 80.7 jit_solution(15521856087270396485)
XLA Ops:
  0.6 78.5 %griffin.1 = (bf16[1536,640]{1,0:T(8,128)(2,1)S(1)}, f32[128,640]{1,0:T(8,128)S(1)}, bf16[3,128,640]{2,1,0:T(8,128)(2,1)S(1)}) custom-call(s32[16]{0:T(128)} %span_ref.1, s32[1,64]{1,0:T(1,128)} %bitcast.8, s32[1,64]{1,0:T(1,128)} %bitcast.9, f32[4,640]{1,0:T(4,128)} %conv_ref.1, f32[640]{0:T(1024)} %rate_ref.1, bf16[1536,2560]{1,0:T(8,128)(2,1)} %tokens_hbm.1, ...), custom_call_target="tpu_custom_call" | custom-call | tf_op jit(solution)/shard_map/griffin/pallas_call | solution.py:757
  79.2 1.6 %write_out.1 = (bf16[1536,640]{1,0:T(8,128)(2,1)}, f32[128,640]{1,0:T(8,128)}, bf16[3,128,640]{2,1,0:T(8,128)(2,1)}) custom-call(bf16[1536,640]{1,0:T(8,128)(2,1)S(1)} %get-tuple-element.9.refs_0_, f32[128,640]{1,0:T(8,128)S(1)} %get-tuple-element.10.refs_1_, bf16[3,128,640]{2,1,0:T(8,128)(2,1)S(1)} %get-tuple-element.11.refs_2_), custom_call_target="tpu_custom_call" | custom-call | tf_op jit(solution)/shard_map/write_out/pallas_call | solution.py:849
